TPU v7x, 32 devices: a whole 2x2x4 slice. The times are simulated.
32 devices in a mesh: groups: 2 (over y), seq: 16 (over z, x, core).
Axes of the slice: x: 2, y: 2, z: 4, core: 2. Of those that a mesh axis runs over, the one named last changes fastest.
Arguments:
- queries: bfloat16 [8192, 2048], P(('groups', 'seq')), parts along dimension 0, may hold values from -6 to 6
- keys: bfloat16 [8192, 2048], P(('groups', 'seq')), parts along dimension 0, may hold values from -0.5390625 to 0.5390625
- values: bfloat16 [8192, 2048], P(('groups', 'seq')), parts along dimension 0, may hold values from -6 to 6
- prompt_state: bfloat16 [16, 2048, 128], P('groups', 'seq'), parts along dimension 0, may hold values from -12 to 12
- lengths: int32 [16], P('groups'), parts along dimension 0, may hold values from 1 to 16, 32 in all
- prompt_of: int32 [16, 1], P('groups'), parts along dimension 0, may hold values from 0 to 7
Outputs:
- mixed: bfloat16 [8192, 2048], P(('groups', 'seq')), parts along dimension 0
There are 2 independent parts, one for each index of `groups`. A program takes and returns all parts, laid end to end along the dimension named above; each array names one. Nothing has to cross between parts.
Inputs may be any that keep to these rules, and one draw needn't show every extreme that they name: `lengths`: responses fill the group's blocks exactly in order; the longest has exactly 16 blocks. `prompt_of`: every prompt has exactly one response.
All inputs are finite; a program needn't handle non-finite values.
Results may differ from a plain program's by a relative error of at most 0.0046.
Values may be sent and summed in bfloat16 or wider, within the bound.
A program may use at most 64 MiB of HBM per device.

v0:
```python
import jax
import jax.numpy as jnp
from jax import lax
from jax.sharding import PartitionSpec as P

DK = 128
DV = 128
SPAN = 128


epsilon = 1e-06


def normalize(mixed):
    scale = lax.rsqrt(jnp.mean(mixed * mixed, axis=-1, keepdims=True) + epsilon)
    return mixed * scale


def shards(queries, keys, values, prompt_state, lengths, prompt_of):
    devices = lax.axis_size("seq")
    position = lax.axis_index("seq")
    tokens = queries.shape[0]
    blocks = tokens // SPAN
    width = queries.shape[1]
    heads = width // DK
    prompts = prompt_state.shape[0]
    starts = jnp.cumsum(lengths) - lengths
    prompt_hot = (prompt_of[:, 0][:, None] == jnp.arange(prompts, dtype=jnp.int32)[None, :]).astype(
        jnp.float32
    )
    own_ids = position * blocks + jnp.arange(blocks, dtype=jnp.int32)
    own_hits = (starts[None, :] == own_ids[:, None]).astype(jnp.float32)
    is_start = jnp.sum(own_hits, axis=1) > 0
    every_state = lax.all_gather(prompt_state, "seq", axis=1, tiled=True)
    own_hot = jnp.dot(own_hits, prompt_hot).astype(jnp.bfloat16)
    cached = jnp.einsum("cp,pre->cre", own_hot, every_state, preferred_element_type=jnp.float32)
    cached = cached.reshape(blocks, heads, DK, DV)
    query_blocks = queries.reshape(blocks, SPAN, heads, DK)
    key_blocks = keys.reshape(blocks, SPAN, heads, DK)
    value_blocks = values.reshape(blocks, SPAN, heads, DV)
    pair_sums = jnp.einsum(
        "cthd,cthe->chde", key_blocks, value_blocks, preferred_element_type=jnp.float32
    )
    running = jnp.zeros((heads, DK, DV), dtype=jnp.float32)
    seen = jnp.zeros((), dtype=bool)
    local_in = []
    untouched = []
    for block in range(blocks):
        running = jnp.where(is_start[block], cached[block], running)
        seen = jnp.logical_or(seen, is_start[block])
        local_in.append(running)
        untouched.append(jnp.logical_not(seen))
        running = running + pair_sums[block]
    row_count = width // devices
    pieces = running.reshape(devices, row_count, DV)
    gathered_rows = lax.all_to_all(pieces, "seq", split_axis=0, concat_axis=0, tiled=True)
    device_ids = jnp.arange(devices, dtype=jnp.int32)
    owner_hits = (starts[None, :] // blocks == device_ids[:, None]).astype(jnp.int32)
    resets = (jnp.sum(owner_hits, axis=1) > 0).astype(jnp.int32)
    counted = jnp.cumsum(resets)
    before = jnp.concatenate([jnp.zeros((1,), dtype=jnp.int32), counted[:-1]])
    linked = jnp.logical_and(
        device_ids[None, :] < device_ids[:, None], counted[None, :] == before[:, None]
    )
    linked = linked.astype(jnp.float32)
    carried_rows = jnp.dot(
        linked, gathered_rows.reshape(devices, row_count * DV), precision=lax.Precision.HIGHEST
    )
    returned = lax.all_to_all(
        carried_rows.reshape(devices, row_count, DV), "seq", split_axis=0, concat_axis=0, tiled=True
    )
    incoming = returned.reshape(heads, DK, DV)
    states = jnp.stack(
        [
            jnp.where(untouched[block], local_in[block] + incoming, local_in[block])
            for block in range(blocks)
        ]
    )
    rounded = states.astype(jnp.bfloat16)
    inter = jnp.einsum("cthd,chde->cthe", query_blocks, rounded, preferred_element_type=jnp.float32)
    scores = jnp.einsum(
        "cthd,cshd->chts", query_blocks, key_blocks, preferred_element_type=jnp.float32
    )
    causal = jnp.tril(jnp.ones((SPAN, SPAN), dtype=bool))
    weights = jnp.where(causal[None, None], scores, 0.0).astype(jnp.bfloat16)
    intra = jnp.einsum("chts,cshe->cthe", weights, value_blocks, preferred_element_type=jnp.float32)
    mixed = normalize(inter + intra).astype(jnp.bfloat16)
    return mixed.reshape(tokens, heads * DV)


def solution(mesh):
    placed = (
        P(("groups", "seq"), None),
        P(("groups", "seq"), None),
        P(("groups", "seq"), None),
        P("groups", "seq", None),
        P("groups"),
        P("groups", None),
    )
    return jax.shard_map(
        shards, mesh=mesh, in_specs=placed, out_specs=P(("groups", "seq"), None), check_vma=False
    )
```

profile of v0, /device:TPU:19, one launch (start us, length us, event | category | flops | bytes accessed | tf_op | source)
XLA Modules:
  0.0 154.7 jit_solution(14662251672486205146)
XLA Ops:
  6.5 1.8 %copy.37 = bf16[8,128,128]{2,0,1:T(8,128)(2,1)} copy(bf16[8,128,128]{2,1,0:T(8,128)(2,1)} %param.9) | data formatting | bytes 524288 | tf_op args[3]
  8.4 0.0 all-gather.2.cloned.1.call-update
  8.4 1.5 copy.52
  9.9 0.0 copy-start.5
  10.0 1.0 copy.47
  11.0 0.2 copy.51
  11.2 0.2 reduce-window.14
  11.4 0.2 fusion.35
  11.6 0.6 fusion.44
  12.2 2.2 %fusion.15 = f32[2,16,128,128]{3,2,1,0:T(8,128)} fusion(bf16[2,128,16,128]{1,3,2,0:T(8,128)(2,1)S(1)} %copy.47, bf16[2,128,16,128]{3,2,1,0:T(8,128)(2,1)S(1)} %bitcast.69), kind=kOutput, calls=%fused_computation.27 | convolution fusion | flops 134217728 | bytes 4194304 | tf_op jit(solution)/shard_map/cthd,cthe->chde/dot_general | solution.py:41
  14.4 45.7 %all-gather.2.cloned.1.call-done = bf16[8,2048,128]{2,0,1:T(8,128)(2,1)} async-done(((bf16[8,128,128]{2,0,1:T(8,128)(2,1)}), bf16[8,2048,128]{2,0,1:T(8,128)(2,1)}) %all-gather.2.cloned.1.call-update) | async-done | bytes 4194320 | tf_op jit(solution)/shard_map/all_gather | solution.py:34
  60.1 4.9 %fusion.22 = f32[2,2048,128]{2,0,1:T(2,128)} fusion(bf16[8,2048,128]{2,0,1:T(8,128)(2,1)} %all-gather.2.cloned.1.call-done, s32[8]{0:T(128)S(1)} %bitcast.79, s32[8]{0:T(128)S(1)} %get-tuple-element.6, s32[2]{0:T(128)S(1)} %iota_add_fusion), kind=kOutput, calls=%fused_computation.32 | convolution fusion | flops 8388960 | bytes 6291528 | tf_op jit(solution)/shard_map/cp,pre->cre/dot_general | solution.py:36
  65.0 5.3 %broadcast_select_fusion = (f32[1,2048,128]{2,0,1:T(1,128)S(1)}, f32[1,2048,128]{2,0,1:T(1,128)S(1)}) fusion(pred[]{:T(512)} %bitcast.2, f32[2,2048,128]{2,0,1:T(2,128)} %fusion.22), kind=kLoop, calls=%fused_computation.4 | loop fusion | flops 262144 | bytes 4194305 | tf_op jit(solution)/shard_map/jit(_where)/select_n | solution.py:49
  70.3 2.2 %fusion.6 = (f32[16,128,128]{2,1,0:T(8,128)}, f32[16,128,128]{2,1,0:T(8,128)}) fusion(f32[2,16,128,128]{3,2,1,0:T(8,128)S(1)} %copy-done.2, f32[16,128,128]{2,1,0:T(8,128)S(1)} %bitcast.73, f32[16,128,128]{2,1,0:T(8,128)S(1)} %bitcast.67, pred[]{:T(512)} %bitcast.8), kind=kLoop, calls=%fused_computation.17 | loop fusion | flops 786432 | bytes 6291457 | tf_op jit(solution)/shard_map/add | solution.py:53
  72.5 6.0 %all-to-all-start = ((f32[16,128,128]{2,1,0:T(8,128)}), f32[16,128,128]{2,1,0:T(8,128)}, u32[]{:S(2)}, u32[]{:S(2)}) async-start(f32[16,128,128]{2,1,0:T(8,128)} %get-tuple-element.7), calls=%async_computation | async-start | bytes 2097152 | tf_op jit(solution)/shard_map/all_to_all | solution.py:56
  78.5 0.1 convert_reduce_fusion
  78.6 0.1 copy.38
  78.7 0.1 reduce
  78.9 0.1 slice_reduce_fusion
  79.0 0.1 pad_add_fusion
  79.1 22.3 %all-to-all-done = f32[16,128,128]{2,1,0:T(8,128)} async-done(((f32[16,128,128]{2,1,0:T(8,128)}), f32[16,128,128]{2,1,0:T(8,128)}, u32[]{:S(2)}, u32[]{:S(2)}) %all-to-all-start) | async-done | bytes 1048608 | tf_op jit(solution)/shard_map/all_to_all | solution.py:56
  101.4 2.4 %fusion.3 = f32[16,128,128]{2,0,1:T(8,128)S(1)} fusion(s32[16]{0:T(128)S(1)} %reduce, s32[16]{0:T(128)S(1)} %pad_add_fusion, f32[2,8,128,128]{3,2,1,0:T(8,128)} %bitcast.25), kind=kOutput, calls=%fused_computation.13 | convolution fusion | flops 50332416 | bytes 2097280 | tf_op jit(solution)/shard_map/dot_general | solution.py:66
  103.8 1.3 copy.42
  105.1 7.0 %all-to-all-start.1 = ((f32[16,128,128]{2,1,0:T(8,128)}), f32[16,128,128]{2,1,0:T(8,128)}, u32[]{:S(2)}, u32[]{:S(2)}) async-start(f32[16,128,128]{2,1,0:T(8,128)} %copy.42), calls=%async_computation.1 | async-start | bytes 2097152 | tf_op jit(solution)/shard_map/all_to_all | solution.py:69
  114.0 2.4 %copy.54 = bf16[32,8,16,128]{3,2,1,0:T(8,128)(2,1)} copy(bf16[32,8,16,128]{3,1,2,0:T(8,128)(2,1)} %bitcast.78) | data formatting | bytes 2097152
  116.4 18.6 %all-to-all-done.1 = f32[16,128,128]{2,1,0:T(8,128)} async-done(((f32[16,128,128]{2,1,0:T(8,128)}), f32[16,128,128]{2,1,0:T(8,128)}, u32[]{:S(2)}, u32[]{:S(2)}) %all-to-all-start.1) | async-done | bytes 1048608 | tf_op jit(solution)/shard_map/all_to_all | solution.py:69
  135.0 1.9 %fusion.24 = (bf16[1,16,128,128]{3,2,1,0:T(8,128)(2,1)S(1)}, bf16[1,16,128,128]{3,2,1,0:T(8,128)(2,1)S(1)}) fusion(f32[16,128,128]{2,1,0:T(8,128)S(1)} %bitcast.68, f32[16,128,128]{2,1,0:T(8,128)} %all-to-all-done.1, pred[]{:T(512)S(6)} %not.6, f32[16,128,128]{2,1,0:T(8,128)} %get-tuple-element.8, pred[]{:T(512)S(6)} %not.7), kind=kLoop, calls=%fused_computation.34 | loop fusion | flops 1572864 | bytes 4194306 | tf_op jit(solution)/shard_map/stack | solution.py:73
  137.0 2.2 %fusion.9 = f32[2,16,128,128]{3,2,1,0:T(8,128)} fusion(bf16[1,16,128,128]{3,2,1,0:T(8,128)(2,1)S(1)} %get-tuple-element.12, bf16[1,16,128,128]{3,2,1,0:T(8,128)(2,1)S(1)} %get-tuple-element.11, bf16[2,128,16,128]{3,2,1,0:T(8,128)(2,1)S(1)} %bitcast.71), kind=kOutput, calls=%fused_computation.21 | convolution fusion | flops 134742016 | bytes 4194304 | tf_op jit(solution)/shard_map/cthd,chde->cthe/dot_general | solution.py:80
  139.2 4.5 %multiply_reduce_fusion = (f32[2,128,16]{1,2,0:T(8,128)S(1)}, f32[2,128,16,128]{1,3,2,0:T(8,128)}) fusion(bf16[2,128,16,128]{1,3,2,0:T(8,128)(2,1)S(1)} %copy.47, pred[128,128]{1,0:T(8,128)(4,1)S(1)} %iota_compare_fusion, bf16[2,128,16,128]{3,2,1,0:T(8,128)(2,1)S(1)} %bitcast.70, bf16[2,128,16,128]{3,2,1,0:T(8,128)(2,1)S(1)} %bitcast.72, ...), kind=kOutput, calls=%fused_computation.2 | convolution fusion | flops 271052800 | bytes 7372800 | tf_op jit(solution)/shard_map/chts,cshe->cthe/dot_general | solution.py:86
  143.8 1.8 %multiply_convert_fusion = bf16[2,128,16,128]{1,3,2,0:T(8,128)(2,1)S(1)} fusion(f32[2,128,16,128]{1,3,2,0:T(8,128)} %get-tuple-element.16, f32[2,128,16]{1,2,0:T(8,128)S(1)} %add_rsqrt_fusion), kind=kLoop, calls=%fused_computation.1 | loop fusion | flops 1048576 | bytes 3162112 | tf_op jit(solution)/shard_map/convert_element_type | solution.py:87
  145.6 1.0 copy.48
  146.6 1.2 copy.78
  (19 shorter events, 0.1 us)
Async XLA Ops:
  6.5 53.5 %all-gather.2.cloned.1.call-start = ((), (), s32[]{:S(2)}) async-start(), calls=%async_computation.2 | async-start | bytes 4456448 | tf_op jit(solution)/shard_map/all_gather | solution.py:34
  8.4 2.6 %copy-start.3 = (bf16[256,2048]{1,0:T(8,128)(2,1)S(1)}, bf16[256,2048]{1,0:T(8,128)(2,1)}, u32[]{:S(2)}) copy-start(bf16[256,2048]{1,0:T(8,128)(2,1)} %param.7) | copy-start | bytes 3145732
  9.9 1.2 copy-start.5
  12.2 47.9 %copy-start.4 = (s32[8,1]{0,1:T(1,128)S(1)}, s32[8,1]{0,1:T(1,128)}, u32[]{:S(2)}) copy-start(s32[8,1]{0,1:T(1,128)} %param.11) | copy-start | bytes 100
  65.0 5.3 %copy-start.2 = (f32[2,16,128,128]{3,2,1,0:T(8,128)S(1)}, f32[2,16,128,128]{3,2,1,0:T(8,128)}, u32[]{:S(2)}) copy-start(f32[2,16,128,128]{3,2,1,0:T(8,128)} %fusion.15) | copy-start | bytes 6291460
  72.5 28.9 %all-to-all-start = ((f32[16,128,128]{2,1,0:T(8,128)}), f32[16,128,128]{2,1,0:T(8,128)}, u32[]{:S(2)}, u32[]{:S(2)}) async-start(f32[16,128,128]{2,1,0:T(8,128)} %get-tuple-element.7), calls=%async_computation | async-start | bytes 2097152 | tf_op jit(solution)/shard_map/all_to_all | solution.py:56
  105.1 29.9 %all-to-all-start.1 = ((f32[16,128,128]{2,1,0:T(8,128)}), f32[16,128,128]{2,1,0:T(8,128)}, u32[]{:S(2)}, u32[]{:S(2)}) async-start(f32[16,128,128]{2,1,0:T(8,128)} %copy.42), calls=%async_computation.1 | async-start | bytes 2097152 | tf_op jit(solution)/shard_map/all_to_all | solution.py:69
  135.0 1.9 %copy-start = (bf16[32,8,16,128]{3,2,1,0:T(8,128)(2,1)S(1)}, bf16[32,8,16,128]{3,2,1,0:T(8,128)(2,1)}, u32[]{:S(2)}) copy-start(bf16[32,8,16,128]{3,2,1,0:T(8,128)(2,1)} %copy.54) | copy-start | bytes 3145732
  137.0 2.3 %copy-start.1 = (bf16[32,8,16,128]{3,2,1,0:T(8,128)(2,1)S(1)}, bf16[32,8,16,128]{3,2,1,0:T(8,128)(2,1)}, u32[]{:S(2)}) copy-start(bf16[32,8,16,128]{3,2,1,0:T(8,128)(2,1)} %copy.54) | copy-start | bytes 3145732
Sparse Core Ops, SparseCore 0:
  9.5 50.5 all-gather.1
where the time goes:
time: 157 us; the launch traced here: 155 us
  waiting for transfers between devices  86.7 us (55%)
  matrix products  16.3 us (10%)
  between operations  15.4 us (10%)
  starting transfers between devices  13.1 us (8%)
  other arithmetic  11.9 us (8%)
  local copies, waits for them, and re-layouts  11.3 us (7%)
    all_gather x1, waiting for transfers between devices, shards(): every_state = lax.all_gather(prompt_state, 'seq', axis=1, tiled=True)  45.7 us
    all_to_all x1, waiting for transfers between devices, shards(): lax.all_to_all(pieces, 'seq', split_axis=0, concat_axis=0, tiled=True)  22.3 us
    all_to_all x1, waiting for transfers between devices, shards(): lax.all_to_all(carried_rows.reshape(devices, row_count, DV), 'seq', split...  18.6 us
    unnamed x17, local copies, waits for them, and re-layouts  7.29 us
    all_to_all x1, starting transfers between devices, shards(): lax.all_to_all(carried_rows.reshape(devices, row_count, DV), 'seq', split...  7.01 us
    all_to_all x1, starting transfers between devices, shards(): lax.all_to_all(pieces, 'seq', split_axis=0, concat_axis=0, tiled=True)  6.05 us
    select_n x1, other arithmetic, shards(): running = jnp.where(is_start[block], cached[block], running)  5.26 us
    dot_general x1, matrix products, shards(): jnp.einsum('cp,pre->cre', own_hot, every_state, preferred_element_type=jn...  4.95 us
  transfers between devices with their start and end apart: 3, of which 3 were waited for; matrix products, arithmetic and copies ran while one was open for 6% of the time, Pallas kernels for 0%

commit v1 on v0

v1 whole, which is shorter than its diff:
```python
import functools
import jax
import jax.numpy as jnp
from jax import lax
from jax.experimental import pallas as pl
from jax.experimental.pallas import tpu as pltpu
from jax.sharding import PartitionSpec as P

DK = 128
DV = 128
SPAN = 128
epsilon = 1e-06


def matmul(a, b, ca, cb):
    return lax.dot_general(a, b, (((ca,), (cb,)), ((), ())), preferred_element_type=jnp.float32)


def kernel(n, q_hbm, k_hbm, v_hbm, p_hbm, len_ref, of_ref, out_hbm,
           q_ref, k_ref, v_ref, p_ref, out_ref, intra, first, sum_out, sum_in, st_out, st_in, pr_out, pr_in,
           index, flag, load_sem, out_sem, sum_send, sum_recv, st_send, st_recv, pr_send, pr_recv):
    me = lax.axis_index("seq")
    width = k_ref.shape[1]
    heads = width // DK
    rows = width // n
    pieces = DK // rows
    responses = len_ref.shape[0]

    def load(i, src, dst):
        return pltpu.make_async_copy(src, dst, load_sem.at[i])

    loads = [load(0, p_hbm, p_ref), load(1, k_hbm, k_ref), load(2, v_hbm, v_ref), load(3, q_hbm, q_ref)]
    for copy in loads:
        copy.start()

    barrier = pltpu.get_barrier_semaphore()

    @pl.loop(1, n)
    def _(j):
        pl.semaphore_signal(barrier, inc=1, device_id={"seq": lax.rem(me + j, n)}, device_id_type=pl.DeviceIdType.MESH)

    @pl.loop(0, 2 * n)
    def _(c):
        start = jnp.int32(0)
        begins = jnp.int32(0)
        which = jnp.int32(0)
        for r in range(responses):
            hit = jnp.where(start == c, 1, 0)
            begins = begins + hit
            which = which + hit * of_ref[r, 0]
            start = start + len_ref[r]
        flag[c] = begins
        index[c] = which

    pl.semaphore_wait(barrier, n - 1)

    def send(src, dst, send_sem, recv_sem, target):
        return pltpu.make_async_remote_copy(
            src_ref=src, dst_ref=dst, send_sem=send_sem, recv_sem=recv_sem,
            device_id={"seq": target}, device_id_type=pl.DeviceIdType.MESH)

    loads[0].wait()

    @pl.loop(1, n + 1)
    def _(j):
        target = lax.rem(me + j, n)
        pr_out[target] = p_ref[index[2 * target + 1]]

        @pl.when(target != me)
        def _():
            send(pr_out.at[target], pr_in.at[me], pr_send, pr_recv, target).start()

    pr_in[me] = pr_out[me]

    loads[1].wait()
    loads[2].wait()
    second_starts = flag[2 * me + 1] > 0
    my_head = me // pieces

    @pl.loop(0, heads)
    def _(i):
        h = lax.rem(my_head + 1 + i, heads)
        cols = pl.ds(pl.multiple_of(h * DK, DK), DK)
        a = matmul(k_ref[0:SPAN, cols], v_ref[0:SPAN, cols], 0, 0)
        b = matmul(k_ref[SPAN:2 * SPAN, cols], v_ref[SPAN:2 * SPAN, cols], 0, 0)
        first[h] = a
        total = jnp.where(second_starts, b, a + b).astype(jnp.bfloat16)
        for j in range(pieces):
            owner = h * pieces + j
            sum_out[owner] = total[j * rows:(j + 1) * rows]

            @pl.when(owner != me)
            def _():
                send(sum_out.at[owner], sum_in.at[me], sum_send, sum_recv.at[me], owner).start()

    sum_in[me] = sum_out[me]

    loads[3].wait()
    causal = lax.broadcasted_iota(jnp.int32, (SPAN, SPAN), 0) >= lax.broadcasted_iota(jnp.int32, (SPAN, SPAN), 1)

    @pl.loop(0, heads)
    def _(h):
        cols = pl.ds(pl.multiple_of(h * DK, DK), DK)
        for block in range(2):
            rng = slice(block * SPAN, (block + 1) * SPAN)
            scores = matmul(q_ref[rng, cols], k_ref[rng, cols], 1, 1)
            weights = jnp.where(causal, scores, 0.0).astype(jnp.bfloat16)
            intra[rng, cols] = matmul(weights, v_ref[rng, cols], 1, 0)

    def scan(d, state):
        state = jnp.where(flag[2 * d] > 0, p_ref[index[2 * d]].astype(jnp.float32), state)
        st_out[d] = state.astype(jnp.bfloat16)

        @pl.when(d != me)
        def _():
            send(st_out.at[d], st_in.at[me], st_send, st_recv.at[me], d).start()
            send(sum_out.at[d], sum_in.at[d], sum_send, sum_recv.at[d], d).wait_recv()

        base = jnp.where(flag[2 * d + 1] > 0, p_ref[index[2 * d + 1]].astype(jnp.float32), state)
        return base + sum_in[d].astype(jnp.float32)

    lax.fori_loop(0, n, scan, jnp.zeros((rows, DV), jnp.float32))
    st_in[me] = st_out[me]

    def others(ref):
        return ref.at[0:n - 1]

    pltpu.make_async_copy(others(pr_in), others(pr_in), pr_recv).wait()

    @pl.loop(0, heads)
    def _(h):
        cols = pl.ds(pl.multiple_of(h * DK, DK), DK)
        for j in range(pieces):
            owner = h * pieces + j

            @pl.when(owner != me)
            def _():
                send(st_out.at[owner], st_in.at[owner], st_send, st_recv.at[owner], owner).wait_recv()

        entering = st_in[pl.ds(h * pieces, pieces)].reshape(DK, DV)
        prompt = pr_in[pl.ds(h * pieces, pieces)].reshape(DK, DV)
        later = (entering.astype(jnp.float32) + first[h]).astype(jnp.bfloat16)
        states = (entering, jnp.where(second_starts, prompt, later))
        for block in range(2):
            rng = slice(block * SPAN, (block + 1) * SPAN)
            o = matmul(q_ref[rng, cols], states[block], 1, 0) + intra[rng, cols]
            scale = lax.rsqrt(jnp.mean(o * o, axis=-1, keepdims=True) + epsilon)
            out_ref[rng, cols] = (o * scale).astype(jnp.bfloat16)
        pltpu.make_async_copy(out_ref.at[:, cols], out_hbm.at[:, cols], out_sem).start()

    pltpu.make_async_copy(out_ref, out_hbm, out_sem).wait()
    pltpu.make_async_copy(others(pr_out), others(pr_out), pr_send).wait()
    pltpu.make_async_copy(others(sum_out), others(sum_out), sum_send).wait()
    pltpu.make_async_copy(others(st_out), others(st_out), st_send).wait()


def solution(mesh):
    n = mesh.shape["seq"]

    def shards(queries, keys, values, prompt_state, lengths, prompt_of):
        tokens, width = queries.shape
        prompts, rows, _ = prompt_state.shape
        half = jnp.bfloat16
        anywhere = pl.BlockSpec(memory_space=pl.ANY)
        scalar = pl.BlockSpec(memory_space=pltpu.SMEM)
        piece = pltpu.VMEM((n, rows, DV), half)
        dma = pltpu.SemaphoreType.DMA
        return pl.pallas_call(
            functools.partial(kernel, n),
            out_shape=jax.ShapeDtypeStruct((tokens, width), half),
            in_specs=[anywhere] * 4 + [scalar] * 2,
            out_specs=anywhere,
            scratch_shapes=[
                pltpu.VMEM((tokens, width), half),
                pltpu.VMEM((tokens, width), half),
                pltpu.VMEM((tokens, width), half),
                pltpu.VMEM((prompts, rows, DV), half),
                pltpu.VMEM((tokens, width), half),
                pltpu.VMEM((tokens, width), jnp.float32),
                pltpu.VMEM((width // DK, DK, DV), jnp.float32),
                piece, piece, piece, piece, piece, piece,
                pltpu.SMEM((2 * n,), jnp.int32),
                pltpu.SMEM((2 * n,), jnp.int32),
                dma((4,)), dma(()),
                dma(()), dma((n,)), dma(()), dma((n,)), dma(()), dma(()),
            ],
            compiler_params=pltpu.CompilerParams(
                collective_id=0, has_side_effects=True, vmem_limit_bytes=62 << 20),
        )(queries, keys, values, prompt_state, lengths, prompt_of)

    placed = (
        P(("groups", "seq"), None),
        P(("groups", "seq"), None),
        P(("groups", "seq"), None),
        P("groups", "seq", None),
        P("groups"),
        P("groups", None),
    )
    return jax.shard_map(
        shards, mesh=mesh, in_specs=placed, out_specs=P(("groups", "seq"), None), check_vma=False
    )
```

time: 157 us -> 47.4 us (0.30)
  waiting for transfers between devices: 86.7 us -> 0 us
  Pallas kernels: 0 us -> 43 us
  matrix products: 16.3 us -> 0 us
  between operations: 15.4 us -> 0.01 us
  starting transfers between devices: 13.1 us -> 0 us
  other arithmetic: 11.9 us -> 0 us
  local copies, waits for them, and re-layouts: 11.3 us -> 3.63 us
    all_gather x1 -> x0, waiting for transfers between devices: 45.7 us -> none  [shards(): every_state = lax.all_gather(prompt_state, 'seq', axis=1, tiled=True)]
    pallas_call x0 -> x1, Pallas kernels: none -> 43 us  [shards(): pl.pallas_call(functools.partial(kernel, n), out_shape=jax.ShapeDtypeStru...]
    all_to_all x2 -> x0, waiting for transfers between devices: 40.9 us -> none  [the longest x1 22.3 us: shards(): lax.all_to_all(pieces, 'seq', split_axis=0, concat_axis=0, tiled=True)]
    dot_general x5 -> x0, matrix products: 16.3 us -> none  [the longest x1 4.95 us: shards(): jnp.einsum('cp,pre->cre', own_hot, every_state, preferred_element_type=jn...]
    all_to_all x2 -> x0, starting transfers between devices: 13.1 us -> none  [the longest x1 7.01 us: shards(): lax.all_to_all(carried_rows.reshape(devices, row_count, DV), 'seq', split...]
    select_n x2 -> x0, other arithmetic: 5.28 us -> none  [the longest x1 5.26 us: shards(): running = jnp.where(is_start[block], cached[block], running)]
    unnamed x17 -> x2, local copies, waits for them, and re-layouts: 7.29 us -> 3.63 us
    another operation x4 -> x0, other arithmetic: 2.26 us -> none  [the longest x1 1.92 us: shards(): jnp.stack([jnp.where(untouched[block], local_in[block] + incoming, local_...]
  transfers between devices with their start and end apart: 3 -> 0, of which waited for: 3 -> 0; matrix products, arithmetic and copies ran while one was open for 6% -> 0% of each run, Pallas kernels for 0% -> 0%
where the time goes in v1:
time: 47.4 us; the launch traced here: 46.6 us
  Pallas kernels  43 us (91%)
  local copies, waits for them, and re-layouts  3.63 us (8%)
    pallas_call x1, Pallas kernels, shards(): pl.pallas_call(functools.partial(kernel, n), out_shape=jax.ShapeDtypeStru...  43 us
    unnamed x2, local copies, waits for them, and re-layouts  3.63 us

profile of v1, /device:TPU:19, one launch (start us, length us, event | category | flops | bytes accessed | tf_op | source)
XLA Modules:
  0.0 46.6 jit_solution(7611032462779572601)
XLA Ops:
  0.0 1.3 %copy.7.of_ref = s32[8,1]{1,0:T(8,128)} copy(s32[8,1]{0,1:T(1,128)} %param.11) | data formatting | bytes 64 | tf_op args[5]
  1.3 43.0 %shard_map.64 = bf16[256,2048]{1,0:T(8,128)(2,1)} custom-call(bf16[256,2048]{1,0:T(8,128)(2,1)} %q_hbm.1, bf16[256,2048]{1,0:T(8,128)(2,1)} %k_hbm.1, bf16[256,2048]{1,0:T(8,128)(2,1)} %v_hbm.1, bf16[8,128,128]{2,1,0:T(8,128)(2,1)} %p_hbm.1, s32[8]{0:T(128)} %len_ref.1, s32[8,1]{1,0:T(8,128)} %copy.7.of_ref), custom_call_target="tpu_custom_call" | custom-call | tf_op jit(solution)/shard_map/pallas_call | solution.py:168
  44.3 2.3 %copy.9 = bf16[256,2048]{1,0:T(8,128)(2,1)} copy(bf16[256,2048]{1,0:T(8,128)(2,1)} %shard_map.64) | data formatting | bytes 2097152

commit v2 on v1

v2 whole, which is shorter than its diff:
```python
import functools
import jax
import jax.numpy as jnp
from jax import lax
from jax.experimental import pallas as pl
from jax.experimental.pallas import tpu as pltpu
from jax.sharding import PartitionSpec as P

DK = 128
DV = 128
SPAN = 128
epsilon = 1e-06


def matmul(a, b, ca, cb):
    return lax.dot_general(a, b, (((ca,), (cb,)), ((), ())), preferred_element_type=jnp.float32)


def kernel(n, q_hbm, k_hbm, v_hbm, p_hbm, len_ref, of_ref, out_hbm,
           q_ref, k_ref, v_ref, own_prompts, far_prompts, out_ref, intra, first, sum_out, sum_in, st_out, st_in, pr_out, pr_in,
           over_out, over_in, index, flag, load_sem, out_sem, swap_sem, over_sem, sum_send, sum_recv, st_send, st_recv,
           pr_send, pr_recv):
    me = lax.axis_index("seq")
    half = n // 2
    side = me // half
    own = lax.rem(me, half)
    base = side * half
    partner = lax.rem(me + half, n)
    width = k_ref.shape[1]
    heads = width // DK
    rows = width // n
    pieces = DK // rows
    responses = len_ref.shape[0]

    def load(i, src, dst):
        return pltpu.make_async_copy(src, dst, load_sem.at[i])

    loads = [load(0, p_hbm, own_prompts), load(1, k_hbm, k_ref), load(2, v_hbm, v_ref), load(3, q_hbm, q_ref)]
    for copy in loads:
        copy.start()

    barrier = pltpu.get_barrier_semaphore()

    def greet(device):
        pl.semaphore_signal(barrier, inc=1, device_id={"seq": device}, device_id_type=pl.DeviceIdType.MESH)

    greet(partner)

    @pl.loop(1, half)
    def _(j):
        greet(base + lax.rem(own + j, half))

    @pl.loop(0, n)
    def _(i):
        c = 2 * base + i
        start = jnp.int32(0)
        begins = jnp.int32(0)
        which = jnp.int32(0)
        for r in range(responses):
            hit = jnp.where(start == c, 1, 0)
            begins = begins + hit
            which = which + hit * of_ref[r]
            start = start + len_ref[r]
        flag[i] = begins
        index[i] = which

    pl.semaphore_wait(barrier, half)

    def send(src, dst, send_sem, recv_sem, target):
        return pltpu.make_async_remote_copy(
            src_ref=src, dst_ref=dst, send_sem=send_sem, recv_sem=recv_sem,
            device_id={"seq": target}, device_id_type=pl.DeviceIdType.MESH)

    loads[0].wait()
    swap = send(own_prompts, far_prompts, swap_sem.at[0], swap_sem.at[1], partner)
    swap.start()

    def give_prompts(slot, prompts):
        @pl.loop(1, half + 1)
        def _(j):
            target = lax.rem(own + j, half)
            pr_out[target, slot] = prompts[index[2 * target + 1]]

            @pl.when(target != own)
            def _():
                send(pr_out.at[target, slot], pr_in.at[own, slot], pr_send, pr_recv, base + target).start()

        pr_in[own, slot] = pr_out[own, slot]

    give_prompts(0, own_prompts)

    loads[1].wait()
    loads[2].wait()
    second_starts = flag[2 * own + 1] > 0

    @pl.loop(0, heads // 2)
    def _(i):
        pair = lax.rem(own // pieces + 1 + i, heads // 2)
        for slot in range(2):
            h = pair + lax.rem(side + slot, 2) * (heads // 2)
            cols = pl.ds(pl.multiple_of(h * DK, DK), DK)
            a = matmul(k_ref[0:SPAN, cols], v_ref[0:SPAN, cols], 0, 0)
            b = matmul(k_ref[SPAN:2 * SPAN, cols], v_ref[SPAN:2 * SPAN, cols], 0, 0)
            first[h] = a
            total = jnp.where(second_starts, b, a + b).astype(jnp.bfloat16)
            for j in range(pieces):
                sum_out[pair * pieces + j, slot] = total[j * rows:(j + 1) * rows]
        for j in range(pieces):
            owner = pair * pieces + j

            @pl.when(owner != own)
            def _():
                send(sum_out.at[owner], sum_in.at[own], sum_send, sum_recv.at[own], base + owner).start()

    sum_in[own] = sum_out[own]

    loads[3].wait()
    causal = lax.broadcasted_iota(jnp.int32, (SPAN, SPAN), 0) >= lax.broadcasted_iota(jnp.int32, (SPAN, SPAN), 1)

    @pl.loop(0, heads)
    def _(h):
        cols = pl.ds(pl.multiple_of(h * DK, DK), DK)
        for block in range(2):
            rng = slice(block * SPAN, (block + 1) * SPAN)
            scores = matmul(q_ref[rng, cols], k_ref[rng, cols], 1, 1)
            weights = jnp.where(causal, scores, 0.0).astype(jnp.bfloat16)
            intra[rng, cols] = matmul(weights, v_ref[rng, cols], 1, 0)

    swap.wait_recv()
    give_prompts(1, far_prompts)

    over = send(over_out, over_in, over_sem.at[0], over_sem.at[1], partner)

    @pl.when(side == 0)
    def _():
        over_in[...] = jnp.zeros_like(over_in)

    @pl.when(side == 1)
    def _():
        over.wait_recv()

    def cached(block):
        which = index[block]
        return jnp.stack([own_prompts[which], far_prompts[which]]).astype(jnp.float32)

    def scan(d, state):
        state = jnp.where(flag[2 * d] > 0, cached(2 * d), state)
        st_out[d] = state.astype(jnp.bfloat16)

        @pl.when(d != own)
        def _():
            send(st_out.at[d], st_in.at[own], st_send, st_recv.at[own], base + d).start()
            send(sum_out.at[d], sum_in.at[d], sum_send, sum_recv.at[d], base + d).wait_recv()

        from_here = jnp.where(flag[2 * d + 1] > 0, cached(2 * d + 1), state)
        return from_here + sum_in[d].astype(jnp.float32)

    last = lax.fori_loop(0, half, scan, over_in[...].astype(jnp.float32))

    @pl.when(side == 0)
    def _():
        over_out[0] = last[1].astype(jnp.bfloat16)
        over_out[1] = last[0].astype(jnp.bfloat16)
        over.start()

    st_in[own] = st_out[own]

    def others(ref):
        return ref.at[0:half - 1]

    pltpu.make_async_copy(others(pr_in), others(pr_in), pr_recv).wait()

    @pl.loop(0, heads // 2)
    def _(pair):
        for j in range(pieces):
            owner = pair * pieces + j

            @pl.when(owner != own)
            def _():
                send(st_out.at[owner], st_in.at[owner], st_send, st_recv.at[owner], base + owner).wait_recv()

        for slot in range(2):
            h = pair + lax.rem(side + slot, 2) * (heads // 2)
            cols = pl.ds(pl.multiple_of(h * DK, DK), DK)
            entering = st_in[pl.ds(pair * pieces, pieces), slot].reshape(DK, DV)
            prompt = pr_in[pl.ds(pair * pieces, pieces), slot].reshape(DK, DV)
            later = (entering.astype(jnp.float32) + first[h]).astype(jnp.bfloat16)
            states = (entering, jnp.where(second_starts, prompt, later))
            for block in range(2):
                rng = slice(block * SPAN, (block + 1) * SPAN)
                o = matmul(q_ref[rng, cols], states[block], 1, 0) + intra[rng, cols]
                scale = lax.rsqrt(jnp.mean(o * o, axis=-1, keepdims=True) + epsilon)
                out_ref[rng, cols] = (o * scale).astype(jnp.bfloat16)
            pltpu.make_async_copy(out_ref.at[:, cols], out_hbm.at[:, cols], out_sem).start()

    pltpu.make_async_copy(out_ref, out_hbm, out_sem).wait()
    swap.wait_send()
    pltpu.make_async_copy(others(pr_out), others(pr_out), pr_send).wait()
    pltpu.make_async_copy(others(sum_out), others(sum_out), sum_send).wait()
    pltpu.make_async_copy(others(st_out), others(st_out), st_send).wait()

    @pl.when(side == 0)
    def _():
        over.wait_send()


def solution(mesh):
    n = mesh.shape["seq"]

    def shards(queries, keys, values, prompt_state, lengths, prompt_of):
        tokens, width = queries.shape
        prompts, rows, _ = prompt_state.shape
        half = jnp.bfloat16
        anywhere = pl.BlockSpec(memory_space=pl.ANY)
        scalar = pl.BlockSpec(memory_space=pltpu.SMEM)
        piece = pltpu.VMEM((n // 2, 2, rows, DV), half)
        dma = pltpu.SemaphoreType.DMA
        return pl.pallas_call(
            functools.partial(kernel, n),
            out_shape=jax.ShapeDtypeStruct((tokens, width), half),
            in_specs=[anywhere] * 4 + [scalar] * 2,
            out_specs=anywhere,
            scratch_shapes=[
                pltpu.VMEM((tokens, width), half),
                pltpu.VMEM((tokens, width), half),
                pltpu.VMEM((tokens, width), half),
                pltpu.VMEM((prompts, rows, DV), half),
                pltpu.VMEM((prompts, rows, DV), half),
                pltpu.VMEM((tokens, width), half),
                pltpu.VMEM((tokens, width), jnp.float32),
                pltpu.VMEM((width // DK, DK, DV), jnp.float32),
                piece, piece, piece, piece, piece, piece,
                pltpu.VMEM((2, rows, DV), half),
                pltpu.VMEM((2, rows, DV), half),
                pltpu.SMEM((n,), jnp.int32),
                pltpu.SMEM((n,), jnp.int32),
                dma((4,)), dma(()), dma((2,)), dma((2,)),
                dma(()), dma((n // 2,)), dma(()), dma((n // 2,)), dma(()), dma(()),
            ],
            compiler_params=pltpu.CompilerParams(
                collective_id=0, has_side_effects=True, vmem_limit_bytes=62 << 20),
        )(queries, keys, values, prompt_state, lengths, prompt_of.reshape(-1))

    placed = (
        P(("groups", "seq"), None),
        P(("groups", "seq"), None),
        P(("groups", "seq"), None),
        P("groups", "seq", None),
        P("groups"),
        P("groups", None),
    )
    return jax.shard_map(
        shards, mesh=mesh, in_specs=placed, out_specs=P(("groups", "seq"), None), check_vma=False
    )
```

time: 47.4 us -> 41 us (0.86)
  the two profiles are of different devices: /device:TPU:19 before, /device:TPU:31 now
where the time goes in v2:
time: 41 us; the launch traced here: 40.8 us
  Pallas kernels  38.5 us (94%)
  local copies, waits for them, and re-layouts  2.3 us (6%)
    pallas_call x1, Pallas kernels, shards(): pl.pallas_call(functools.partial(kernel, n), out_shape=jax.ShapeDtypeStru...  38.5 us
    unnamed x1, local copies, waits for them, and re-layouts  2.3 us

profile of v2, /device:TPU:31, one launch (start us, length us, event | category | flops | bytes accessed | tf_op | source)
XLA Modules:
  0.0 40.8 jit_solution(2690748942952372298)
XLA Ops:
  0.0 38.5 %shard_map.64 = bf16[256,2048]{1,0:T(8,128)(2,1)} custom-call(bf16[256,2048]{1,0:T(8,128)(2,1)} %q_hbm.1, bf16[256,2048]{1,0:T(8,128)(2,1)} %k_hbm.1, bf16[256,2048]{1,0:T(8,128)(2,1)} %v_hbm.1, bf16[8,128,128]{2,1,0:T(8,128)(2,1)} %p_hbm.1, s32[8]{0:T(128)} %len_ref.1, s32[8]{0:T(128)} %bitcast.1), custom_call_target="tpu_custom_call" | custom-call | tf_op jit(solution)/shard_map/pallas_call | solution.py:218
  38.5 2.3 %copy.8 = bf16[256,2048]{1,0:T(8,128)(2,1)} copy(bf16[256,2048]{1,0:T(8,128)(2,1)} %shard_map.64) | data formatting | bytes 2097152

commit v3 on v2

--- a/solution.py
+++ b/solution.py
@@ -18,7 +18,7 @@
 
 def kernel(n, q_hbm, k_hbm, v_hbm, p_hbm, len_ref, of_ref, out_hbm,
            q_ref, k_ref, v_ref, own_prompts, far_prompts, out_ref, intra, first, sum_out, sum_in, st_out, st_in, pr_out, pr_in,
-           over_out, over_in, index, flag, load_sem, out_sem, swap_sem, over_sem, sum_send, sum_recv, st_send, st_recv,
+           over_out, over_in, index, flag, load_sem, out_sem, swap_sem, over_send, over_recv, sum_send, sum_recv, st_send, st_recv,
            pr_send, pr_recv):
     me = lax.axis_index("seq")
     half = n // 2
@@ -83,7 +83,7 @@
 
             @pl.when(target != own)
             def _():
-                send(pr_out.at[target, slot], pr_in.at[own, slot], pr_send, pr_recv, base + target).start()
+                send(pr_out.at[target, slot], pr_in.at[own, slot], pr_send, pr_recv.at[slot], base + target).start()
 
         pr_in[own, slot] = pr_out[own, slot]
 
@@ -117,69 +117,93 @@
     loads[3].wait()
     causal = lax.broadcasted_iota(jnp.int32, (SPAN, SPAN), 0) >= lax.broadcasted_iota(jnp.int32, (SPAN, SPAN), 1)
 
-    @pl.loop(0, heads)
-    def _(h):
-        cols = pl.ds(pl.multiple_of(h * DK, DK), DK)
-        for block in range(2):
-            rng = slice(block * SPAN, (block + 1) * SPAN)
-            scores = matmul(q_ref[rng, cols], k_ref[rng, cols], 1, 1)
-            weights = jnp.where(causal, scores, 0.0).astype(jnp.bfloat16)
-            intra[rng, cols] = matmul(weights, v_ref[rng, cols], 1, 0)
-
+    def within(low, high):
+        @pl.loop(low, high)
+        def _(h):
+            cols = pl.ds(pl.multiple_of(h * DK, DK), DK)
+            for block in range(2):
+                rng = slice(block * SPAN, (block + 1) * SPAN)
+                scores = matmul(q_ref[rng, cols], k_ref[rng, cols], 1, 1)
+                weights = jnp.where(causal, scores, 0.0).astype(jnp.bfloat16)
+                intra[rng, cols] = matmul(weights, v_ref[rng, cols], 1, 0)
+
+    within(0, heads // 2)
+
+    @pl.loop(1, half)
+    def _(j):
+        d = lax.rem(own + half - j, half)
+        send(sum_out.at[d], sum_in.at[d], sum_send, sum_recv.at[d], base + d).wait_recv()
+
+    def scan(slot, prompts, state):
+        def step(d, state):
+            state = jnp.where(flag[2 * d] > 0, prompts[index[2 * d]].astype(jnp.float32), state)
+            st_out[d, slot] = state.astype(jnp.bfloat16)
+            state = jnp.where(flag[2 * d + 1] > 0, prompts[index[2 * d + 1]].astype(jnp.float32), state)
+            return state + sum_in[d, slot].astype(jnp.float32)
+
+        return lax.fori_loop(0, half, step, state)
+
+    def give_states(slot):
+        @pl.loop(1, half)
+        def _(j):
+            d = lax.rem(own + j, half)
+            send(st_out.at[d, slot], st_in.at[own, slot], st_send, st_recv.at[slot, own], base + d).start()
+
+        st_in[own, slot] = st_out[own, slot]
+
+    def over(slot):
+        return send(over_out.at[slot], over_in.at[1 - slot], over_send.at[slot], over_recv.at[1 - slot], partner)
+
+    def arrived(slot):
+        over(1 - slot).wait_recv()
+        return over_in[slot].astype(jnp.float32)
+
+    def hand_over(slot, state):
+        over_out[slot] = state.astype(jnp.bfloat16)
+        over(slot).start()
+
+    nothing = jnp.zeros((rows, DV), jnp.float32)
+
+    @pl.when(side == 0)
+    def _():
+        hand_over(0, scan(0, own_prompts, nothing))
+        give_states(0)
+
+    within(heads // 2, heads)
     swap.wait_recv()
-    give_prompts(1, far_prompts)
-
-    over = send(over_out, over_in, over_sem.at[0], over_sem.at[1], partner)
 
     @pl.when(side == 0)
     def _():
-        over_in[...] = jnp.zeros_like(over_in)
+        hand_over(1, scan(1, far_prompts, nothing))
+        give_states(1)
+        give_prompts(1, far_prompts)
 
     @pl.when(side == 1)
     def _():
-        over.wait_recv()
-
-    def cached(block):
-        which = index[block]
-        return jnp.stack([own_prompts[which], far_prompts[which]]).astype(jnp.float32)
-
-    def scan(d, state):
-        state = jnp.where(flag[2 * d] > 0, cached(2 * d), state)
-        st_out[d] = state.astype(jnp.bfloat16)
-
-        @pl.when(d != own)
-        def _():
-            send(st_out.at[d], st_in.at[own], st_send, st_recv.at[own], base + d).start()
-            send(sum_out.at[d], sum_in.at[d], sum_send, sum_recv.at[d], base + d).wait_recv()
-
-        from_here = jnp.where(flag[2 * d + 1] > 0, cached(2 * d + 1), state)
-        return from_here + sum_in[d].astype(jnp.float32)
-
-    last = lax.fori_loop(0, half, scan, over_in[...].astype(jnp.float32))
-
-    @pl.when(side == 0)
-    def _():
-        over_out[0] = last[1].astype(jnp.bfloat16)
-        over_out[1] = last[0].astype(jnp.bfloat16)
-        over.start()
-
-    st_in[own] = st_out[own]
+        scan(1, far_prompts, arrived(1))
+        give_states(1)
+        give_prompts(1, far_prompts)
+        scan(0, own_prompts, arrived(0))
+        give_states(0)
 
     def others(ref):
         return ref.at[0:half - 1]
 
-    pltpu.make_async_copy(others(pr_in), others(pr_in), pr_recv).wait()
-
-    @pl.loop(0, heads // 2)
-    def _(pair):
-        for j in range(pieces):
-            owner = pair * pieces + j
-
-            @pl.when(owner != own)
-            def _():
-                send(st_out.at[owner], st_in.at[owner], st_send, st_recv.at[owner], base + owner).wait_recv()
-
-        for slot in range(2):
+    @pl.loop(0, 2)
+    def _(turn):
+        slot = lax.rem(side + turn, 2)
+        pltpu.make_async_copy(pr_in.at[0:half - 1, 0], pr_in.at[0:half - 1, 0], pr_recv.at[slot]).wait()
+
+        @pl.loop(0, heads // 2)
+        def _(i):
+            pair = lax.rem(own // pieces + heads // 2 - i, heads // 2)
+            for j in range(pieces):
+                owner = pair * pieces + j
+
+                @pl.when(owner != own)
+                def _():
+                    send(st_out.at[owner, slot], st_in.at[owner, slot], st_send, st_recv.at[slot, owner], base + owner).wait_recv()
+
             h = pair + lax.rem(side + slot, 2) * (heads // 2)
             cols = pl.ds(pl.multiple_of(h * DK, DK), DK)
             entering = st_in[pl.ds(pair * pieces, pieces), slot].reshape(DK, DV)
@@ -201,7 +225,8 @@
 
     @pl.when(side == 0)
     def _():
-        over.wait_send()
+        over(0).wait_send()
+        over(1).wait_send()
 
 
 def solution(mesh):
@@ -234,8 +259,8 @@
                 pltpu.VMEM((2, rows, DV), half),
                 pltpu.SMEM((n,), jnp.int32),
                 pltpu.SMEM((n,), jnp.int32),
-                dma((4,)), dma(()), dma((2,)), dma((2,)),
-                dma(()), dma((n // 2,)), dma(()), dma((n // 2,)), dma(()), dma(()),
+                dma((4,)), dma(()), dma((2,)), dma((2,)), dma((2,)),
+                dma(()), dma((n // 2,)), dma(()), dma((2, n // 2)), dma(()), dma((2,)),
             ],
             compiler_params=pltpu.CompilerParams(
                 collective_id=0, has_side_effects=True, vmem_limit_bytes=62 << 20),

time: 41 us -> 38.6 us (0.941)
  the two profiles are of different devices: /device:TPU:31 before, /device:TPU:19 now
where the time goes in v3:
time: 38.6 us; the launch traced here: 37.8 us
  Pallas kernels  35.5 us (92%)
  local copies, waits for them, and re-layouts  2.3 us (6%)
    pallas_call x1, Pallas kernels, shards(): pl.pallas_call(functools.partial(kernel, n), out_shape=jax.ShapeDtypeStru...  35.5 us
    unnamed x1, local copies, waits for them, and re-layouts  2.3 us

profile of v3, /device:TPU:19, one launch (start us, length us, event | category | flops | bytes accessed | tf_op | source)
XLA Modules:
  0.0 37.8 jit_solution(1080677799987890162)
XLA Ops:
  0.0 35.5 %shard_map.64 = bf16[256,2048]{1,0:T(8,128)(2,1)} custom-call(bf16[256,2048]{1,0:T(8,128)(2,1)} %q_hbm.1, bf16[256,2048]{1,0:T(8,128)(2,1)} %k_hbm.1, bf16[256,2048]{1,0:T(8,128)(2,1)} %v_hbm.1, bf16[8,128,128]{2,1,0:T(8,128)(2,1)} %p_hbm.1, s32[8]{0:T(128)} %len_ref.1, s32[8]{0:T(128)} %bitcast.1), custom_call_target="tpu_custom_call" | custom-call | tf_op jit(solution)/shard_map/pallas_call | solution.py:243
  35.5 2.3 %copy.8 = bf16[256,2048]{1,0:T(8,128)(2,1)} copy(bf16[256,2048]{1,0:T(8,128)(2,1)} %shard_map.64) | data formatting | bytes 2097152

commit v4 on v3

--- a/solution.py
+++ b/solution.py
@@ -87,8 +87,6 @@
 
         pr_in[own, slot] = pr_out[own, slot]
 
-    give_prompts(0, own_prompts)
-
     loads[1].wait()
     loads[2].wait()
     second_starts = flag[2 * own + 1] > 0
@@ -127,12 +125,11 @@
                 weights = jnp.where(causal, scores, 0.0).astype(jnp.bfloat16)
                 intra[rng, cols] = matmul(weights, v_ref[rng, cols], 1, 0)
 
-    within(0, heads // 2)
-
-    @pl.loop(1, half)
-    def _(j):
-        d = lax.rem(own + half - j, half)
-        send(sum_out.at[d], sum_in.at[d], sum_send, sum_recv.at[d], base + d).wait_recv()
+    def sums_arrived():
+        @pl.loop(1, half)
+        def _(j):
+            d = lax.rem(own + half - j, half)
+            send(sum_out.at[d], sum_in.at[d], sum_send, sum_recv.at[d], base + d).wait_recv()
 
     def scan(slot, prompts, state):
         def step(d, state):
@@ -164,25 +161,25 @@
 
     nothing = jnp.zeros((rows, DV), jnp.float32)
 
+    give_prompts(0, own_prompts)
+    within(0, heads)
+    sums_arrived()
+
     @pl.when(side == 0)
     def _():
         hand_over(0, scan(0, own_prompts, nothing))
         give_states(0)
-
-    within(heads // 2, heads)
-    swap.wait_recv()
-
-    @pl.when(side == 0)
-    def _():
+        swap.wait_recv()
         hand_over(1, scan(1, far_prompts, nothing))
         give_states(1)
         give_prompts(1, far_prompts)
 
     @pl.when(side == 1)
     def _():
+        swap.wait_recv()
+        give_prompts(1, far_prompts)
         scan(1, far_prompts, arrived(1))
         give_states(1)
-        give_prompts(1, far_prompts)
         scan(0, own_prompts, arrived(0))
         give_states(0)
 

time: 38.6 us -> 34.8 us (0.902)
  the two profiles are of different devices: /device:TPU:19 before, /device:TPU:0 now
where the time goes in v4:
time: 34.8 us; the launch traced here: 34.7 us
  Pallas kernels  32.4 us (93%)
  local copies, waits for them, and re-layouts  2.3 us (7%)
    pallas_call x1, Pallas kernels, shards(): pl.pallas_call(functools.partial(kernel, n), out_shape=jax.ShapeDtypeStru...  32.4 us
    unnamed x1, local copies, waits for them, and re-layouts  2.3 us

profile of v4, /device:TPU:0, one launch (start us, length us, event | category | flops | bytes accessed | tf_op | source)
XLA Modules:
  0.0 34.7 jit_solution(4374324749958321959)
XLA Ops:
  0.0 32.4 %shard_map.64 = bf16[256,2048]{1,0:T(8,128)(2,1)} custom-call(bf16[256,2048]{1,0:T(8,128)(2,1)} %q_hbm.1, bf16[256,2048]{1,0:T(8,128)(2,1)} %k_hbm.1, bf16[256,2048]{1,0:T(8,128)(2,1)} %v_hbm.1, bf16[8,128,128]{2,1,0:T(8,128)(2,1)} %p_hbm.1, s32[8]{0:T(128)} %len_ref.1, s32[8]{0:T(128)} %bitcast.1), custom_call_target="tpu_custom_call" | custom-call | tf_op jit(solution)/shard_map/pallas_call | solution.py:240
  32.4 2.3 %copy.8 = bf16[256,2048]{1,0:T(8,128)(2,1)} copy(bf16[256,2048]{1,0:T(8,128)(2,1)} %shard_map.64) | data formatting | bytes 2097152

commit v5 on v4

--- a/solution.py
+++ b/solution.py
@@ -171,8 +171,8 @@
         give_states(0)
         swap.wait_recv()
         hand_over(1, scan(1, far_prompts, nothing))
+        give_prompts(1, far_prompts)
         give_states(1)
-        give_prompts(1, far_prompts)
 
     @pl.when(side == 1)
     def _():

time: 34.8 us -> 33.7 us (0.968)
  the two profiles are of different devices: /device:TPU:0 before, /device:TPU:19 now
where the time goes in v5:
time: 33.7 us; the launch traced here: 33.1 us
  Pallas kernels  30.8 us (91%)
  local copies, waits for them, and re-layouts  2.3 us (7%)
    pallas_call x1, Pallas kernels, shards(): pl.pallas_call(functools.partial(kernel, n), out_shape=jax.ShapeDtypeStru...  30.8 us
    unnamed x1, local copies, waits for them, and re-layouts  2.3 us

profile of v5, /device:TPU:19, one launch (start us, length us, event | category | flops | bytes accessed | tf_op | source)
XLA Modules:
  0.0 33.1 jit_solution(15836240673400548779)
XLA Ops:
  0.0 30.8 %shard_map.64 = bf16[256,2048]{1,0:T(8,128)(2,1)} custom-call(bf16[256,2048]{1,0:T(8,128)(2,1)} %q_hbm.1, bf16[256,2048]{1,0:T(8,128)(2,1)} %k_hbm.1, bf16[256,2048]{1,0:T(8,128)(2,1)} %v_hbm.1, bf16[8,128,128]{2,1,0:T(8,128)(2,1)} %p_hbm.1, s32[8]{0:T(128)} %len_ref.1, s32[8]{0:T(128)} %bitcast.1), custom_call_target="tpu_custom_call" | custom-call | tf_op jit(solution)/shard_map/pallas_call | solution.py:240
  30.8 2.3 %copy.8 = bf16[256,2048]{1,0:T(8,128)(2,1)} copy(bf16[256,2048]{1,0:T(8,128)(2,1)} %shard_map.64) | data formatting | bytes 2097152

commit v6 on v5

--- a/solution.py
+++ b/solution.py
@@ -170,8 +170,8 @@
         hand_over(0, scan(0, own_prompts, nothing))
         give_states(0)
         swap.wait_recv()
+        give_prompts(1, far_prompts)
         hand_over(1, scan(1, far_prompts, nothing))
-        give_prompts(1, far_prompts)
         give_states(1)
 
     @pl.when(side == 1)

time: 33.7 us -> 35 us (1.039)
  Pallas kernels: 30.8 us -> 32.5 us
    pallas_call x1, Pallas kernels: 30.8 us -> 32.5 us  [shards(): pl.pallas_call(functools.partial(kernel, n), out_shape=jax.ShapeDtypeStru...]
where the time goes in v6:
time: 35 us; the launch traced here: 34.8 us
  Pallas kernels  32.5 us (93%)
  local copies, waits for them, and re-layouts  2.3 us (7%)
    pallas_call x1, Pallas kernels, shards(): pl.pallas_call(functools.partial(kernel, n), out_shape=jax.ShapeDtypeStru...  32.5 us
    unnamed x1, local copies, waits for them, and re-layouts  2.3 us

profile of v6, /device:TPU:19, one launch (start us, length us, event | category | flops | bytes accessed | tf_op | source)
XLA Modules:
  0.0 34.8 jit_solution(240031271436786629)
XLA Ops:
  0.0 32.5 %shard_map.64 = bf16[256,2048]{1,0:T(8,128)(2,1)} custom-call(bf16[256,2048]{1,0:T(8,128)(2,1)} %q_hbm.1, bf16[256,2048]{1,0:T(8,128)(2,1)} %k_hbm.1, bf16[256,2048]{1,0:T(8,128)(2,1)} %v_hbm.1, bf16[8,128,128]{2,1,0:T(8,128)(2,1)} %p_hbm.1, s32[8]{0:T(128)} %len_ref.1, s32[8]{0:T(128)} %bitcast.1), custom_call_target="tpu_custom_call" | custom-call | tf_op jit(solution)/shard_map/pallas_call | solution.py:240
  32.5 2.3 %copy.8 = bf16[256,2048]{1,0:T(8,128)(2,1)} copy(bf16[256,2048]{1,0:T(8,128)(2,1)} %shard_map.64) | data formatting | bytes 2097152
